TPU v7x, 256 devices: a whole 4x4x8 slice. The times are simulated.
256 devices in a mesh: req: 32 (over x, z_hi, core), tp: 8 (over y, z_lo).
Axes of the slice: x: 4, y: 4, z: 8 (z_hi: 4, z_lo: 2; z = z_hi * 2 + z_lo), core: 2. Of those that a mesh axis runs over, the one named last changes fastest.
Arguments:
- queries: bfloat16 [8192, 5120], P('req', 'tp')
- suffix_keys: bfloat16 [8192, 5120], P('req', 'tp')
- suffix_values: bfloat16 [8192, 5120], P('req', 'tp'), may hold values from -6 to 6
- page_cache: bfloat16 [64, 128, 2, 5120], P('req', None, None, 'tp'), may hold values from -6 to 6
- page_table: int32 [2, 32], replicated, may hold values from 0 to 63, as said below
- suffix_lengths: int32 [32, 4], P('req'), may hold values from 1 to 128, 256 in all within a row
- request_group: int32 [32, 4], P('req'), may hold values from 0 to 1
- residual: bfloat16 [8192, 5120], P('req', 'tp'), may hold values from -6 to 6
- out_weight: bfloat16 [5120, 5120], P('tp'), may hold values from -0.3125 to 0.3125
- attn_gate: float32 [5120], P('tp'), may hold values from 0.5 to 2
- mod_shift: float32 [5120], P('tp'), may hold values from -3 to 3
- mod_scale: float32 [5120], P('tp'), may hold values from -0.5 to 1
Outputs:
- stream: bfloat16 [8192, 5120], P('req', 'tp')
- mlp_input: bfloat16 [8192, 5120], P('req', 'tp')
Inputs may be any that keep to these rules, and one draw needn't show every extreme that they name: `page_table`: every slot 0 to 63 appears exactly once; slot s lies on req index s // 2. `suffix_lengths`: the lengths of one req index's requests sum to 256.
All inputs are finite; a program needn't handle non-finite values.
Results may differ from a plain program's by a relative error of at most 0.015.
Values may be sent and summed in bfloat16 or wider, within the bound.
No kernel may reach another device: no remote copies, remote signals or barrier semaphores. Data moves between devices by JAX's collectives and lax.ppermute only.
A program may use at most 128 MiB of HBM per device.

v0:
```python
import math
import jax
import jax.numpy as jnp
from jax import lax
from jax.sharding import PartitionSpec as P

D = 5120
HS = 128
SPAN = 64


def body(
    queries,
    suffix_keys,
    suffix_values,
    page_cache,
    page_table,
    suffix_lengths,
    request_group,
    residual,
    out_weight,
    attn_gate,
    mod_shift,
    mod_scale,
):
    tok_count = queries.shape[0]
    local_heads = queries.shape[1] // HS
    page_size = page_cache.shape[1]
    group_count = page_table.shape[0]
    page_count = page_table.shape[1]
    slot_total = group_count * page_count
    inv_sqrt = 1.0 / math.sqrt(HS)
    slot_ids = jnp.arange(slot_total, dtype=jnp.int32)
    table_group = jnp.arange(slot_total, dtype=jnp.int32) // page_count
    matches = page_table.reshape(-1)[:, None] == slot_ids[None, :]
    slot_group = jnp.sum(jnp.where(matches, table_group[:, None], 0), 0)
    positions = jnp.arange(tok_count, dtype=jnp.int32)
    lengths_row = suffix_lengths[0]
    request_ends = jnp.cumsum(lengths_row, dtype=jnp.int32)
    request_starts = request_ends - lengths_row
    token_request = jnp.sum((positions[:, None] >= request_ends[None, :]).astype(jnp.int32), 1)
    choose = token_request[:, None] == jnp.arange(suffix_lengths.shape[1], dtype=jnp.int32)[None, :]
    token_group = jnp.sum(jnp.where(choose, request_group[0][None, :], 0), 1)
    token_start = jnp.sum(jnp.where(choose, request_starts[None, :], 0), 1)
    token_block = (positions - token_start) // SPAN
    query_heads = queries.reshape(tok_count, local_heads, HS)
    key_heads = suffix_keys.reshape(tok_count, local_heads, HS)
    value_heads = suffix_values.reshape(tok_count, local_heads, HS)
    same_request = (token_request[:, None] == token_request[None, :]) & (
        token_block[None, :] <= token_block[:, None]
    )
    scores = (
        jnp.einsum("qhd,khd->hqk", query_heads, key_heads, preferred_element_type=jnp.float32)
        * inv_sqrt
    )
    scores = jnp.where(same_request[None], scores, -1e30)
    largest = jnp.max(scores, -1)
    expo = jnp.where(same_request[None], jnp.exp(scores - largest[..., None]), 0.0)
    denominator = jnp.sum(expo, -1)
    weighted = jnp.einsum(
        "hqk,khd->hqd", expo.astype(jnp.bfloat16), value_heads, preferred_element_type=jnp.float32
    )
    own_state = (largest, denominator, weighted)
    shard_block = lax.all_gather(page_cache, "req", axis=0, tiled=True)
    slot_number = shard_block.shape[0]
    step = math.gcd(slot_number, 4)
    block_count = slot_number // step
    blocks = shard_block.reshape(block_count, step, page_size, 2, local_heads * HS)
    block_starts = step * jnp.arange(block_count, dtype=jnp.int32)

    def one_block(carried, item):
        block, block_start = item
        key_rows = block[:, :, 0, :].reshape(step * page_size, local_heads, HS)
        value_rows = block[:, :, 1, :].reshape(step * page_size, local_heads, HS)
        key_group = jnp.repeat(lax.dynamic_slice_in_dim(slot_group, block_start, step), page_size)
        visible = token_group[:, None] == key_group[None, :]
        max_old, sum_old, acc_old = carried
        page_scores = (
            jnp.einsum("qhd,khd->hqk", query_heads, key_rows, preferred_element_type=jnp.float32)
            * inv_sqrt
        )
        page_scores = jnp.where(visible[None], page_scores, -1e30)
        max_new = jnp.maximum(max_old, jnp.max(page_scores, -1))
        page_expo = jnp.where(visible[None], jnp.exp(page_scores - max_new[..., None]), 0.0)
        factor = jnp.exp(max_old - max_new)
        sum_new = sum_old * factor + jnp.sum(page_expo, -1)
        acc_new = acc_old * factor[..., None] + jnp.einsum(
            "hqk,khd->hqd",
            page_expo.astype(jnp.bfloat16),
            value_rows,
            preferred_element_type=jnp.float32,
        )
        return ((max_new, sum_new, acc_new), None)

    result, unused = lax.scan(one_block, own_state, (blocks, block_starts))
    max_all, sum_all, acc_all = result
    attention = (
        (acc_all / sum_all[..., None])
        .transpose(1, 0, 2)
        .reshape(tok_count, local_heads * HS)
        .astype(jnp.bfloat16)
    )
    projected = (
        lax.psum_scatter(
            lax.dot_general(
                out_weight, attention, (((0,), (1,)), ((), ())), preferred_element_type=jnp.float32
            ).astype(jnp.bfloat16),
            "tp",
            scatter_dimension=0,
            tiled=True,
        )
        .astype(jnp.float32)
        .T
    )
    combined = residual.astype(jnp.float32) + attn_gate[None, :] * projected
    sum_first, sum_second = lax.psum((jnp.sum(combined, 1), jnp.sum(combined * combined, 1)), "tp")
    mean_value = sum_first / D
    variance = sum_second / D - mean_value * mean_value
    normed = (combined - mean_value[:, None]) / jnp.sqrt(variance[:, None] + 1e-06)
    mlp_input = normed * (1.0 + mod_scale[None, :]) + mod_shift[None, :]
    return (combined.astype(jnp.bfloat16), mlp_input.astype(jnp.bfloat16))


def solution(mesh):
    in_specs = (
        P("req", "tp"),
        P("req", "tp"),
        P("req", "tp"),
        P("req", None, None, "tp"),
        P(),
        P("req", None),
        P("req", None),
        P("req", "tp"),
        P("tp", None),
        P("tp"),
        P("tp"),
        P("tp"),
    )
    out_specs = (P("req", "tp"), P("req", "tp"))
    return jax.shard_map(body, mesh=mesh, in_specs=in_specs, out_specs=out_specs, check_vma=False)
```

profile of v0, /device:TPU:2, one launch (start us, length us, event | category | flops | bytes accessed | tf_op | source)
XLA Modules:
  0.0 477.4 jit_solution(15765563890964449459)
XLA Ops:
  7.3 2.1 copy.68
  15.2 128.3 %all-gather.2.cloned.1.call-done = bf16[64,128,2,640]{3,1,2,0:T(8,128)(2,1)} async-done(((bf16[2,128,2,640]{3,1,2,0:T(8,128)(2,1)}), bf16[64,128,2,640]{3,1,2,0:T(8,128)(2,1)}) %all-gather.2.cloned.1.call-update) | async-done | bytes 20971536 | tf_op jit(solution)/shard_map/all_gather | solution.py:64
  143.5 225.4 %while.14 = (s32[]{:T(128)}, f32[5,256]{1,0:T(8,128)S(1)}, f32[5,256]{1,0:T(8,128)S(1)}, f32[5,256,128]{2,1,0:T(8,128)}, s32[256]{0:T(256)S(1)}, /*index=5*/s32[...) while((s32[]{:T(128)}, f32[5,256]{1,0:T(8,128)S(1)}, ...), condition=%wide.region_10.11_spmd, body=%wide.region_7.10_spmd.sunk | while | flops 344525312 | bytes 21910748 | solution.py:95
  150.8 1.8 fusion.48
  154.4 3.2 fusion.50
  168.5 3.2 fusion.50
  182.6 3.2 fusion.50
  196.7 3.2 fusion.50
  210.7 3.2 fusion.50
  224.8 3.2 fusion.50
  238.9 3.2 fusion.50
  253.0 3.2 fusion.50
  267.1 3.2 fusion.50
  281.2 3.2 fusion.50
  295.3 3.2 fusion.50
  309.3 3.2 fusion.50
  323.4 3.2 fusion.50
  337.5 3.2 fusion.50
  351.6 3.2 fusion.50
  365.7 3.2 fusion.50
  370.2 5.1 %fusion.12 = bf16[5120,256]{0,1:T(8,128)(2,1)S(1)} fusion(bf16[256,640]{0,1:T(8,128)(2,1)S(1)} %bitcast.80, bf16[640,5120]{1,0:T(8,128)(2,1)} %param.22), kind=kOutput, calls=%fused_computation.17 | convolution fusion | flops 1679032320 | bytes 9502720 | tf_op jit(solution)/shard_map/dot_general | solution.py:105
  375.4 2.6 copy.79
  378.6 72.4 %reduce-scatter.4.cloned.1.call-done = bf16[640,256]{1,0:T(8,128)(2,1)} async-done(((bf16[5120,256]{1,0:T(8,128)(2,1)}), bf16[640,256]{1,0:T(8,128)(2,1)}) %reduce-scatter.4.cloned.1.call-update) | async-done | bytes 327696
  452.5 17.0 %all-reduce = (f32[256]{0:T(256)S(1)}, f32[256]{0:T(256)S(1)}) all-reduce(f32[256]{0:T(256)S(1)} %get-tuple-element.89, f32[256]{0:T(256)S(1)} %get-tuple-element.88), channel_id=1, replica_groups=mesh['req'=32,'tp'=8] {'tp'}, use_global_device_ids=true, to_apply=%region_15.16 | all-reduce | flops 512 | bytes 4096 | tf_op jit(solution)/shard_map/psum | solution.py:116
  (269 shorter events, 152.9 us)
Async XLA Ops:
  7.2 5.8 %copy-start.8 = (s32[1,4]{1,0:T(1,128)S(1)}, s32[1,4]{1,0:T(1,128)}, u32[]{:S(2)}) copy-start(s32[1,4]{1,0:T(1,128)} %param.19) | copy-start | bytes 52
  7.2 4.2 copy-start.1
  7.2 4.4 copy-start.2
  7.2 5.4 %copy-start.7 = (s32[2,32]{1,0:T(2,128)S(1)}, s32[2,32]{1,0:T(2,128)}, u32[]{:S(2)}) copy-start(s32[2,32]{1,0:T(2,128)} %param.18) | copy-start | bytes 772
  7.2 5.7 %copy-start.6 = (s32[1,4]{1,0:T(1,128)S(1)}, s32[1,4]{1,0:T(1,128)}, u32[]{:S(2)}) copy-start(s32[1,4]{1,0:T(1,128)} %param.20) | copy-start | bytes 52
  7.2 136.3 %all-gather.2.cloned.1.call-start = ((), (), s32[]{:S(2)}) async-start(), calls=%async_computation.1 | async-start | bytes 21626880 | tf_op jit(solution)/shard_map/all_gather | solution.py:64
  9.3 441.7 %reduce-scatter.4.cloned.1.call-start = ((), (), s32[]{:S(2)}) async-start(), calls=%async_computation.2 | async-start | bytes 2949120
  377.9 0.7 copy-start.4
  377.9 74.3 %copy-start = (bf16[256,640]{1,0:T(8,128)(2,1)S(1)}, bf16[256,640]{1,0:T(8,128)(2,1)}, u32[]{:S(2)}) copy-start(bf16[256,640]{1,0:T(8,128)(2,1)} %param.21) | copy-start | bytes 983044
  377.9 74.3 %copy-start.3 = (f32[640]{0:T(1024)S(1)}, f32[640]{0:T(1024)}, u32[]{:S(2)}) copy-start(f32[640]{0:T(1024)} %param.23) | copy-start | bytes 7684
  377.9 91.5 %copy-start.5 = (f32[640]{0:T(1024)S(1)}, f32[640]{0:T(1024)}, u32[]{:S(2)}) copy-start(f32[640]{0:T(1024)} %param.24) | copy-start | bytes 7684
Sparse Core Ops, SparseCore 0:
  10.6 132.8 all-gather.1
  378.1 72.8 reduce-scatter.3
where the time goes:
time: 479 us; the launch traced here: 477 us
  waiting for transfers between devices  201 us (42%)
  local copies, waits for them, and re-layouts  113 us (24%)
  matrix products  86.8 us (18%)
  loops' own time  30.4 us (6%)
  blocking collectives  17 us (4%)
  other arithmetic  15.7 us (3%)
  between operations  14.2 us (3%)
    all_gather x1, waiting for transfers between devices, body(): shard_block = lax.all_gather(page_cache, 'req', axis=0, tiled=True)  128 us
    unnamed x3, waiting for transfers between devices  72.4 us
    dynamic_slice x48, local copies, waits for them, and re-layouts, body(): result, unused = lax.scan(one_block, own_state, (blocks, block_starts))  57.7 us
    dot_general x16, matrix products, one_block(): jnp.einsum('hqk,khd->hqd', page_expo.astype(jnp.bfloat16), value_rows, pr...  50.7 us
    another operation x1, loops' own time, body(): result, unused = lax.scan(one_block, own_state, (blocks, block_starts))  30.4 us
    dot_general x16, matrix products, one_block(): jnp.einsum('qhd,khd->hqk', query_heads, key_rows, preferred_element_type=...  29.3 us
    squeeze x16, local copies, waits for them, and re-layouts, one_block(): key_rows = block[:, :, 0, :].reshape(step * page_size, local_heads, HS)  17.4 us
    squeeze x16, local copies, waits for them, and re-layouts, one_block(): value_rows = block[:, :, 1, :].reshape(step * page_size, local_heads, HS)  17.4 us
  transfers between devices with their start and end apart: 2, of which 2 were waited for; matrix products, arithmetic and copies ran while one was open for 1% of the time, Pallas kernels for 0%

commit v1 on v0

--- a/solution.py
+++ b/solution.py
@@ -7,6 +7,13 @@
 D = 5120
 HS = 128
 SPAN = 64
+
+
+def exchange_gather(array, name, d):
+    n_dev = lax.axis_size(name)
+    tiles = jnp.stack([array for _ in range(n_dev)])
+    tiles = lax.all_to_all(tiles, name, split_axis=0, concat_axis=0)
+    return jnp.concatenate(tiles, axis=d)
 
 
 def body(
@@ -61,7 +68,7 @@
         "hqk,khd->hqd", expo.astype(jnp.bfloat16), value_heads, preferred_element_type=jnp.float32
     )
     own_state = (largest, denominator, weighted)
-    shard_block = lax.all_gather(page_cache, "req", axis=0, tiled=True)
+    shard_block = exchange_gather(page_cache, "req", 0)
     slot_number = shard_block.shape[0]
     step = math.gcd(slot_number, 4)
     block_count = slot_number // step

time: 479 us -> 813 us (1.70)
  waiting for transfers between devices: 201 us -> 517 us
  starting transfers between devices: 0.08 us -> 11.8 us
    all_to_all x0 -> x1, waiting for transfers between devices: none -> 448 us  [exchange_gather(): tiles = lax.all_to_all(tiles, name, split_axis=0, concat_axis=0)]
    all_gather x1 -> x0, waiting for transfers between devices: 128 us -> none  [body(): shard_block = lax.all_gather(page_cache, 'req', axis=0, tiled=True)]
    all_to_all x0 -> x1, starting transfers between devices: none -> 11.8 us  [exchange_gather(): tiles = lax.all_to_all(tiles, name, split_axis=0, concat_axis=0)]
    unnamed x3 -> x2, waiting for transfers between devices: 72.4 us -> 68.7 us
where the time goes in v1:
time: 813 us; the launch traced here: 811 us
  waiting for transfers between devices  517 us (64%)
  local copies, waits for them, and re-layouts  119 us (15%)
  matrix products  87.1 us (11%)
  loops' own time  30.4 us (4%)
  blocking collectives  17 us (2%)
  other arithmetic  15 us (2%)
  between operations  14.2 us (2%)
  starting transfers between devices  11.8 us (1%)
    all_to_all x1, waiting for transfers between devices, exchange_gather(): tiles = lax.all_to_all(tiles, name, split_axis=0, concat_axis=0)  448 us
    unnamed x2, waiting for transfers between devices  68.7 us
    dynamic_slice x48, local copies, waits for them, and re-layouts, body(): result, unused = lax.scan(one_block, own_state, (blocks, block_starts))  57.7 us
    dot_general x16, matrix products, one_block(): jnp.einsum('hqk,khd->hqd', page_expo.astype(jnp.bfloat16), value_rows, pr...  50.9 us
    another operation x1, loops' own time, body(): result, unused = lax.scan(one_block, own_state, (blocks, block_starts))  30.4 us
    dot_general x16, matrix products, one_block(): jnp.einsum('qhd,khd->hqk', query_heads, key_rows, preferred_element_type=...  29.3 us
    squeeze x16, local copies, waits for them, and re-layouts, one_block(): key_rows = block[:, :, 0, :].reshape(step * page_size, local_heads, HS)  17.4 us
    squeeze x16, local copies, waits for them, and re-layouts, one_block(): value_rows = block[:, :, 1, :].reshape(step * page_size, local_heads, HS)  17.4 us
  transfers between devices with their start and end apart: 2, of which 2 were waited for; matrix products, arithmetic and copies ran while one was open for 1% of the time, Pallas kernels for 0%

profile of v1, /device:TPU:2, one launch (start us, length us, event | category | flops | bytes accessed | tf_op | source)
XLA Modules:
  0.0 811.4 jit_solution(14619319780856494959)
XLA Ops:
  8.3 8.1 %stack.2 = bf16[32,2,128,2,640]{4,2,3,1,0:T(8,128)(2,1)} broadcast(bf16[2,128,2,640]{3,1,2,0:T(8,128)(2,1)S(1)} %copy.68), dimensions={1,2,3,4} | broadcast | bytes 21626880 | tf_op jit(solution)/shard_map/stack | solution.py:14
  16.5 11.8 %all-to-all-start = ((bf16[32,2,128,2,640]{4,2,3,1,0:T(8,128)(2,1)}), bf16[32,2,128,2,640]{4,2,3,1,0:T(8,128)(2,1)}, u32[]{:S(2)}, u32[]{:S(2)}) async-start(bf16[32,2,128,2,640]{4,2,3,1,0:T(8,128)(2,1)} %stack.2), calls=%async_computation | async-start | bytes 41943040 | tf_op jit(solution)/shard_map/all_to_all | solution.py:15
  32.6 448.4 %all-to-all-done = bf16[32,2,128,2,640]{4,2,3,1,0:T(8,128)(2,1)} async-done(((bf16[32,2,128,2,640]{4,2,3,1,0:T(8,128)(2,1)}), bf16[32,2,128,2,640]{4,2,3,1,0:T(8,128)(2,1)}, u32[]{:S(2)}, u32[]{:S(2)}) %all-to-all-start) | async-done | bytes 20971552 | tf_op jit(solution)/shard_map/all_to_all | solution.py:15
  481.0 225.6 %while.14 = (s32[]{:T(128)}, f32[5,256]{1,0:T(8,128)S(1)}, f32[5,256]{1,0:T(8,128)S(1)}, f32[5,256,128]{2,1,0:T(8,128)}, s32[256]{0:T(256)S(1)}, /*index=5*/s32[...) while((s32[]{:T(128)}, f32[5,256]{1,0:T(8,128)S(1)}, ...), condition=%wide.region_10.11_spmd, body=%wide.region_7.10_spmd.sunk | while | flops 344525312 | bytes 21910748 | solution.py:102
  491.9 3.2 fusion.50
  506.0 3.2 fusion.50
  520.1 3.2 fusion.50
  534.2 3.2 fusion.50
  548.3 3.2 fusion.50
  562.4 3.2 fusion.50
  576.5 3.2 fusion.50
  590.6 3.2 fusion.50
  604.7 3.2 fusion.50
  618.8 3.2 fusion.50
  632.9 3.2 fusion.50
  647.0 3.2 fusion.50
  661.1 3.2 fusion.50
  675.2 3.2 fusion.50
  689.3 3.2 fusion.50
  703.4 3.2 fusion.50
  707.9 5.1 fusion.12
  713.1 2.6 copy.79
  716.3 68.7 %reduce-scatter.4.cloned.1.call-done = bf16[640,256]{1,0:T(8,128)(2,1)} async-done(((bf16[5120,256]{1,0:T(8,128)(2,1)}), bf16[640,256]{1,0:T(8,128)(2,1)}) %reduce-scatter.4.cloned.1.call-update) | async-done | bytes 327696
  786.5 17.0 %all-reduce = (f32[256]{0:T(256)S(1)}, f32[256]{0:T(256)S(1)}) all-reduce(f32[256]{0:T(256)S(1)} %get-tuple-element.89, f32[256]{0:T(256)S(1)} %get-tuple-element.88), channel_id=1, replica_groups=mesh['req'=32,'tp'=8] {'tp'}, use_global_device_ids=true, to_apply=%region_15.16 | all-reduce | flops 512 | bytes 4096 | tf_op jit(solution)/shard_map/psum | solution.py:123
  (271 shorter events, 154.2 us)
Async XLA Ops:
  16.4 11.9 %copy-start.9 = (s32[1,4]{1,0:T(1,128)S(1)}, s32[1,4]{1,0:T(1,128)}, u32[]{:S(2)}) copy-start(s32[1,4]{1,0:T(1,128)} %param.19) | copy-start | bytes 52
  16.4 12.1 %copy-start.1 = (bf16[256,640]{1,0:T(8,128)(2,1)S(1)}, bf16[256,640]{1,0:T(8,128)(2,1)}, u32[]{:S(2)}) copy-start(bf16[256,640]{1,0:T(8,128)(2,1)} %param.14) | copy-start | bytes 983044
  16.5 12.3 %copy-start.2 = (bf16[256,640]{1,0:T(8,128)(2,1)S(1)}, bf16[256,640]{1,0:T(8,128)(2,1)}, u32[]{:S(2)}) copy-start(bf16[256,640]{1,0:T(8,128)(2,1)} %param.15) | copy-start | bytes 983044
  16.5 12.5 %copy-start.3 = (bf16[256,640]{1,0:T(8,128)(2,1)S(1)}, bf16[256,640]{1,0:T(8,128)(2,1)}, u32[]{:S(2)}) copy-start(bf16[256,640]{1,0:T(8,128)(2,1)} %param.16) | copy-start | bytes 983044
  16.5 464.5 %all-to-all-start = ((bf16[32,2,128,2,640]{4,2,3,1,0:T(8,128)(2,1)}), bf16[32,2,128,2,640]{4,2,3,1,0:T(8,128)(2,1)}, u32[]{:S(2)}, u32[]{:S(2)}) async-start(bf16[32,2,128,2,640]{4,2,3,1,0:T(8,128)(2,1)} %stack.2), calls=%async_computation | async-start | bytes 41943040 | tf_op jit(solution)/shard_map/all_to_all | solution.py:15
  28.3 1.7 copy-start.8
  28.3 2.0 copy-start.7
  28.3 756.7 %reduce-scatter.4.cloned.1.call-start = ((), (), s32[]{:S(2)}) async-start(), calls=%async_computation.2 | async-start | bytes 2949120
  715.6 0.7 copy-start.5
  715.6 70.6 %copy-start = (bf16[256,640]{1,0:T(8,128)(2,1)S(1)}, bf16[256,640]{1,0:T(8,128)(2,1)}, u32[]{:S(2)}) copy-start(bf16[256,640]{1,0:T(8,128)(2,1)} %param.21) | copy-start | bytes 983044
  715.6 70.6 %copy-start.4 = (f32[640]{0:T(1024)S(1)}, f32[640]{0:T(1024)}, u32[]{:S(2)}) copy-start(f32[640]{0:T(1024)} %param.23) | copy-start | bytes 7684
  715.6 87.8 %copy-start.6 = (f32[640]{0:T(1024)S(1)}, f32[640]{0:T(1024)}, u32[]{:S(2)}) copy-start(f32[640]{0:T(1024)} %param.24) | copy-start | bytes 7684
Sparse Core Ops, SparseCore 0:
  715.8 69.2 reduce-scatter.3
